TPU v7x, 32 devices: a whole 2x2x4 slice. The times are simulated.
32 devices in a mesh: blk: 8 (over y, x, core), cross: 4 (over z).
Axes of the slice: x: 2, y: 2, z: 4, core: 2. Of those that a mesh axis runs over, the one named last changes fastest.
Arguments:
- receiver_spectra: float32 [4096, 2, 1024], P(('blk', 'cross')), may hold values from -400 to 400
- source_spectra: float32 [4096, 2, 1024], P(('blk', 'cross')), may hold values from -400 to 400
- quality: int32 [4096], P(('blk', 'cross')), may hold values 0 or 1
- slot_order: int32 [32, 128], P(('blk', 'cross')), may hold values from 0 to 127, each once within a row
- owners: int32 [2, 8], replicated, may hold values from 0 to 3
Outputs:
- correlations: bfloat16 [2, 8, 4, 128, 128, 256], P(None, 'blk', 'cross')
Inputs may be any that keep to these rules, and one draw needn't show every extreme that they name: `slot_order`: each row is a permutation of 0 to 127.
All inputs are finite; a program needn't handle non-finite values. No bound on the sum of `quality` on one device may be relied on, other than what follows from the above.
Results may differ from a plain program's by a relative error of at most 0.0056.
Values sent between devices are 32-bit elements; how exact they have to be, the bound alone decides.
A program may use at most 128 MiB of HBM per device.

v0:
```python
import math

import jax
import jax.numpy as jnp
from jax import lax
from jax.sharding import PartitionSpec as P

L = 256
STEPS = 2


def passed_along(value, axis, steps):
    count = lax.axis_size(axis)
    pairs = [(source, (source + steps) % count) for source in range(count)]
    return lax.ppermute(value, axis, pairs)


def lag_tables(bins, lags):
    bin_index = jnp.arange(bins, dtype=jnp.int32)
    odd_index = 2 * jnp.arange(lags // 2, dtype=jnp.int32) + 1
    phase_turns = jnp.mod(bin_index[:, None] * odd_index[None, :], 4 * bins).astype(jnp.float32)
    phase_angle = phase_turns * (math.pi / (2 * bins))
    cos_table = (jnp.cos(phase_angle) / bins).astype(jnp.bfloat16)
    sin_table = (-jnp.sin(phase_angle) / bins).astype(jnp.bfloat16)
    return (cos_table, sin_table)


def whiten(spectra):
    mean_power = jnp.mean(spectra * spectra, axis=(1, 2), keepdims=True)
    return spectra * lax.rsqrt(mean_power + 1e-06)


def correlate(panel_spec, slab_spec, cos_table, sin_table):
    npanel = panel_spec.shape[0]
    nslab = slab_spec.shape[0]
    width = math.gcd(npanel, 16)
    blocks = panel_spec.reshape(npanel // width, width, 2, panel_spec.shape[2])

    def one_block(source):
        inphase = (
            source[:, None, 0, :] * slab_spec[None, :, 0, :]
            + source[:, None, 1, :] * slab_spec[None, :, 1, :]
        )
        quadrature = (
            source[:, None, 1, :] * slab_spec[None, :, 0, :]
            - source[:, None, 0, :] * slab_spec[None, :, 1, :]
        )
        inphase = inphase.astype(jnp.bfloat16).reshape(width * nslab, -1)
        quadrature = quadrature.astype(jnp.bfloat16).reshape(width * nslab, -1)
        even = jnp.dot(inphase, cos_table, preferred_element_type=jnp.float32)
        odd = jnp.dot(quadrature, sin_table, preferred_element_type=jnp.float32)
        joined = jnp.concatenate([even + odd, even - odd], axis=-1).astype(jnp.bfloat16)
        return joined.reshape(width, nslab, -1)

    lagged = lax.map(one_block, blocks)
    return lagged.reshape(npanel, nslab, lagged.shape[-1])


def local(receiver_spectra, source_spectra, quality, slot_order, owners):
    bins = receiver_spectra.shape[2]
    npanel = source_spectra.shape[0]
    cos_table, sin_table = lag_tables(bins, L)
    kept = quality.astype(jnp.float32)[:, None, None]
    receivers = whiten(receiver_spectra) * kept
    receivers = jnp.take(receivers, slot_order[0], axis=0)
    sources = whiten(source_spectra)
    block_index = lax.axis_index("blk")
    my_owners = lax.dynamic_index_in_dim(owners, block_index, 1, keepdims=False)
    every_panel = lax.all_gather(sources, "cross", axis=0, tiled=True)
    moving = receivers
    results = []
    for loop_step in range(STEPS):
        if loop_step > 0:
            moving = passed_along(moving, "blk", 1)
        owner_index = my_owners[loop_step]
        panel_spec = lax.dynamic_slice_in_dim(every_panel, owner_index * npanel, npanel, 0)
        results.append(correlate(panel_spec, moving, cos_table, sin_table))
    return jnp.stack(results)[:, None, None]


def solution(mesh):
    placed = (
        P(("blk", "cross"), None, None),
        P(("blk", "cross"), None, None),
        P(("blk", "cross")),
        P(("blk", "cross"), None),
        P(),
    )
    return jax.shard_map(
        local,
        mesh=mesh,
        in_specs=placed,
        out_specs=P(None, "blk", "cross", None, None, None),
        check_vma=False,
    )
```

profile of v0, /device:TPU:0, one launch (start us, length us, event | category | flops | bytes accessed | tf_op | source)
XLA Modules:
  0.0 305.8 jit_solution(16467009084390342149)
XLA Ops:
  21.7 73.5 %all-gather.2.cloned.1.call-done = f32[512,2,1024]{2,1,0:T(2,128)} async-done(((f32[128,2,1024]{2,1,0:T(2,128)}), f32[512,2,1024]{2,1,0:T(2,128)}) %all-gather.2.cloned.1.call-update) | async-done | bytes 4194320 | tf_op jit(solution)/shard_map/all_gather | solution.py:69
  95.1 3.2 %constant_dynamic-slice_fusion.1 = (f32[128,2,1024]{2,1,0:T(2,128)S(1)}, f32[128,2,1024]{2,1,0:T(2,128)}) fusion(f32[512,2,1024]{2,1,0:T(2,128)} %all-gather.2.cloned.1.call-done, s32[]{:T(128)S(6)} %select_n.44, s32[]{:T(128)S(6)} %select_n.49), kind=kLoop, calls=%fused_computation.86 | loop fusion | bytes 4194312 | tf_op jit(solution)/shard_map/dynamic_slice | solution.py:76
  98.4 4.3 %broadcast.91.clone = bf16[8,16,128,256]{3,2,1,0:T(8,128)(2,1)} broadcast(bf16[]{:T(256)} %constant.66.clone.1), dimensions={} | broadcast | bytes 8388610 | tf_op jit(solution)/shard_map/broadcast.6
  102.6 92.7 %while.25 = (s32[]{:T(128)}, bf16[8,16,128,256]{3,2,1,0:T(8,128)(2,1)}, f32[8,16,2,1024]{3,2,1,0:T(2,128)}, f32[128,2,1024]{2,1,0:T(2,128)S(1)}, s32[128]{0:T(128)S(1)}, /*index=5*/s32[]{:T(128)}) while((s32[]{:T(128)}, bf16[8,16,128,256]{3,2,1,0:T(8,128)(2,1)}, f32[8,16,2,1024]{3,2,1,0:T(2,128)}, ...), condition=%wide.region_5.6_spmd.clone.clone, body=%wide.region_4.5_spmd.clone.clone.sunk | while | flops 1097990144 | bytes 28181588 | solution.py:55
  104.7 2.7 subtract_convert_fusion.7
  107.4 2.9 fusion.81
  110.3 2.8 add_convert_fusion.7
  116.3 2.7 subtract_convert_fusion.7
  119.0 2.9 fusion.81
  121.8 2.8 add_convert_fusion.7
  127.9 2.7 subtract_convert_fusion.7
  130.6 2.9 fusion.81
  133.4 2.8 add_convert_fusion.7
  139.5 2.7 subtract_convert_fusion.7
  142.1 2.9 fusion.81
  145.0 2.8 add_convert_fusion.7
  151.1 2.7 subtract_convert_fusion.7
  153.7 2.9 fusion.81
  156.6 2.8 add_convert_fusion.7
  162.6 2.7 subtract_convert_fusion.7
  165.3 2.9 fusion.81
  168.2 2.8 add_convert_fusion.7
  174.2 2.7 subtract_convert_fusion.7
  176.9 2.9 fusion.81
  179.8 2.8 add_convert_fusion.7
  185.8 2.7 subtract_convert_fusion.7
  188.5 2.9 fusion.81
  191.4 2.8 add_convert_fusion.7
  195.4 4.3 %broadcast.91.clone.1 = bf16[8,16,128,256]{3,2,1,0:T(8,128)(2,1)} broadcast(bf16[]{:T(256)} %constant.66.clone.1), dimensions={} | broadcast | bytes 8388610 | tf_op jit(solution)/shard_map/broadcast.6
  199.7 85.5 %while.24 = (s32[]{:T(128)}, bf16[8,16,128,256]{3,2,1,0:T(8,128)(2,1)}, f32[8,16,2,1024]{3,2,1,0:T(2,128)S(1)}, f32[128,2,1024]{2,1,0:T(2,128)S(1)}, s32[128]{0:T(128)S(1)}, /*index=5*/s32[]{:T(128)}) while((s32[]{:T(128)}, bf16[8,16,128,256]{3,2,1,0:T(8,128)(2,1)}, f32[8,16,2,1024]{3,2,1,0:T(2,128)S(1)}, ...), condition=%wide.region_3.4_spmd.clone.clone, body=%wide.region_2.3_spmd.clone.clone.sunk | while | flops 1097990144 | bytes 28181588 | solution.py:55
  203.5 2.9 fusion.76
  206.4 2.8 add_convert_fusion.6
  214.3 2.9 fusion.76
  217.1 2.8 add_convert_fusion.6
  224.9 2.9 fusion.76
  227.8 2.8 add_convert_fusion.6
  232.9 2.7 subtract_convert_fusion.6
  235.6 2.9 fusion.76
  238.5 2.8 add_convert_fusion.6
  246.3 2.9 fusion.76
  249.2 2.8 add_convert_fusion.6
  257.0 2.9 fusion.76
  259.9 2.8 add_convert_fusion.6
  267.7 2.9 fusion.76
  270.5 2.8 add_convert_fusion.6
  278.3 2.9 fusion.76
  281.2 2.8 add_convert_fusion.6
  285.2 13.8 %maximum_bitcast_fusion = bf16[2,1,1,128,128,256]{5,4,3,2,1,0:T(8,128)(2,1)} fusion(bf16[1,128,128,256]{3,2,1,0:T(8,128)(2,1)} %bitcast.87, bf16[1,128,128,256]{3,2,1,0:T(8,128)(2,1)} %bitcast.86), kind=kLoop, calls=%fused_computation.75 | loop fusion | flops 8388608 | bytes 33554432 | tf_op jit(solution)/shard_map/broadcast_in_dim | solution.py:78
  (128 shorter events, 76.5 us)
Async XLA Ops:
  6.5 13.2 %copy-start = (s32[2,8]{1,0:T(2,128)S(1)}, s32[2,8]{1,0:T(2,128)}, u32[]{:S(2)}) copy-start(s32[2,8]{1,0:T(2,128)} %param.13) | copy-start | bytes 196
  6.5 11.9 %copy-start.2 = (s32[1,128]{1,0:T(1,128)S(1)}, s32[1,128]{1,0:T(1,128)}, u32[]{:S(2)}) copy-start(s32[1,128]{1,0:T(1,128)} %param.12) | copy-start | bytes 1540
  6.5 88.6 %all-gather.2.cloned.1.call-start = ((), (), s32[]{:S(2)}) async-start(), calls=%async_computation | async-start | bytes 5242880 | tf_op jit(solution)/shard_map/all_gather | solution.py:69
  19.0 79.3 %collective-permute-start = (f32[128,2,1024]{2,1,0:T(2,128)S(1)}, f32[128,2,1024]{2,1,0:T(2,128)S(1)}, u32[]{:S(2)}, u32[]{:S(2)}) collective-permute-start(f32[128,2,1024]{2,1,0:T(2,128)S(1)} %broadcast_select_fusion), channel_id=1, source_target_pairs={{0,4},{4,8},{8,12},{12,16},{16,20},{20,24},{24,28},{28,0},{1,5},{5... | collective-permute-start | bytes 3145736 | tf_op jit(solution)/shard_map/ppermute | solution.py:15
  285.2 13.8 %copy-start.1 = (s32[2,8]{1,0:T(2,128)S(1)}, s32[2,8]{1,0:T(2,128)}, u32[]{:S(2)}) copy-start(s32[2,8]{1,0:T(2,128)} %param.13) | copy-start | bytes 196
Sparse Core Ops, SparseCore 0:
  11.6 83.4 all-gather.1
where the time goes:
time: 306 us
  matrix products  90.8 us (30%)
  other arithmetic  85.6 us (28%)
  waiting for transfers between devices  73.5 us (24%)
  local copies, waits for them, and re-layouts  39.7 us (13%)
  between operations  14.7 us (5%)
    all_gather x1, waiting for transfers between devices, local(): every_panel = lax.all_gather(sources, 'cross', axis=0, tiled=True)  73.5 us
    dot_general x16, matrix products, one_block(): odd = jnp.dot(quadrature, sin_table, preferred_element_type=jnp.float32)  45.8 us
    dot_general x16, matrix products, one_block(): even = jnp.dot(inphase, cos_table, preferred_element_type=jnp.float32)  45 us
    convert_element_type x16, other arithmetic, one_block(): quadrature = quadrature.astype(jnp.bfloat16).reshape(width * nslab, -1)  42.7 us
    dynamic_update_slice x16, other arithmetic, correlate(): lagged = lax.map(one_block, blocks)  18.4 us
    broadcast_in_dim x1, other arithmetic, local(): return jnp.stack(results)[:, None, None]  13.8 us
    slice x16, local copies, waits for them, and re-layouts, one_block(): slab_spec[None, :, 0, :]  13 us
    another operation x2, local copies, waits for them, and re-layouts  8.57 us
  transfers between devices with their start and end apart: 2, of which 1 were waited for; matrix products, arithmetic and copies ran while one was open for 4% of the time, Pallas kernels for 0%

commit v1 on v0

v1 whole, which is shorter than its diff:
```python
import functools
import math

import jax
import jax.numpy as jnp
import numpy as np
from jax import lax
from jax.experimental import pallas as pl
from jax.experimental.pallas import tpu as pltpu
from jax.sharding import PartitionSpec as P

L = 256
STEPS = 2
FINE = 16


def phase_tables(bins, coarse):
    bin_index = np.arange(bins, dtype=np.float64)[None, :]
    fine_angle = np.pi / bins * (np.arange(FINE)[:, None] + 0.5) * bin_index
    coarse_angle = np.pi / bins * (FINE * np.arange(coarse)[:, None]) * bin_index
    fine = np.stack([np.cos(fine_angle), np.sin(fine_angle)])
    slow = np.stack([np.cos(coarse_angle), np.sin(coarse_angle)]) / bins
    return jnp.asarray(fine, jnp.float32), jnp.asarray(slow, jnp.float32)


def whiten(spectra):
    mean_power = jnp.mean(spectra * spectra, axis=(1, 2), keepdims=True)
    return spectra * lax.rsqrt(mean_power + 1e-06)


def build_columns(slab, slow_ref, w_ref):
    bins = slow_ref.shape[2]
    slots = slab.shape[0]
    real, imag = slab[:, :bins], slab[:, bins:]
    for a in range(slow_ref.shape[1]):
        c, s = slow_ref[0, a : a + 1, :], slow_ref[1, a : a + 1, :]
        rc, rs, ic, is_ = real * c, real * s, imag * c, imag * s
        rows = slice(a * slots, (a + 1) * slots)
        w_ref[0, rows, :bins] = (rc + is_).astype(jnp.bfloat16)
        w_ref[0, rows, bins:] = (ic - rs).astype(jnp.bfloat16)
        w_ref[1, rows, :bins] = (rc - is_).astype(jnp.bfloat16)
        w_ref[1, rows, bins:] = (ic + rs).astype(jnp.bfloat16)


def build_rows(panel, fine_ref, x_ref):
    bins = fine_ref.shape[2]
    c, s = fine_ref[0], fine_ref[1]
    for p in range(panel.shape[0]):
        real, imag = panel[p : p + 1, :bins], panel[p : p + 1, bins:]
        rc, rs, ic, is_ = real * c, real * s, imag * c, imag * s
        rows = slice(p * FINE, (p + 1) * FINE)
        x_ref[0, rows, :bins] = (rc - is_).astype(jnp.bfloat16)
        x_ref[0, rows, bins:] = (rs + ic).astype(jnp.bfloat16)
        x_ref[1, rows, :bins] = (rc + is_).astype(jnp.bfloat16)
        x_ref[1, rows, bins:] = (ic - rs).astype(jnp.bfloat16)


def products(x_ref, w_ref, out_ref, channels, slots, coarse):
    half = coarse * FINE
    for sign in range(2):
        found = lax.dot_general(
            x_ref[sign], w_ref[sign], (((1,), (1,)), ((), ())), preferred_element_type=jnp.float32
        )
        for p in range(channels):
            part = found[p * FINE : (p + 1) * FINE]
            lags = jnp.concatenate([part[:, a * slots : (a + 1) * slots] for a in range(coarse)], axis=0)
            out_ref[p, :, sign * half : (sign + 1) * half] = lags.T.astype(jnp.bfloat16)


def kernel(coarse, s_ref, q_ref, fine_ref, slow_ref, out_ref, w_ref, x_ref):
    slots = q_ref.shape[1]
    channels = s_ref.shape[1]

    @pl.when(pl.program_id(1) == 0)
    def _():
        build_columns(q_ref[0], slow_ref, w_ref)

    build_rows(s_ref[0], fine_ref, x_ref)
    products(x_ref, w_ref, out_ref.at[0], channels, slots, coarse)


def correlate(panels, slabs, channels=16):
    steps, npanel, width = panels.shape
    nslab = slabs.shape[1]
    coarse = L // 2 // FINE
    fine, slow = phase_tables(width // 2, coarse)
    return pl.pallas_call(
        functools.partial(kernel, coarse),
        grid=(steps, npanel // channels),
        in_specs=[
            pl.BlockSpec((1, channels, width), lambda s, i: (s, i, 0)),
            pl.BlockSpec((1, nslab, width), lambda s, i: (s, 0, 0)),
            pl.BlockSpec(fine.shape, lambda s, i: (0, 0, 0)),
            pl.BlockSpec(slow.shape, lambda s, i: (0, 0, 0)),
        ],
        out_specs=pl.BlockSpec((1, channels, nslab, L), lambda s, i: (s, i, 0, 0)),
        out_shape=jax.ShapeDtypeStruct((steps, npanel, nslab, L), jnp.bfloat16),
        scratch_shapes=[
            pltpu.VMEM((2, coarse * nslab, width), jnp.bfloat16),
            pltpu.VMEM((2, channels * FINE, width), jnp.bfloat16),
        ],
        compiler_params=pltpu.CompilerParams(vmem_limit_bytes=56 << 20),
    )(panels, slabs, fine, slow)


def passed_along(value, axis, steps):
    count = lax.axis_size(axis)
    pairs = [(source, (source + steps) % count) for source in range(count)]
    return lax.ppermute(value, axis, pairs)


def local(receiver_spectra, source_spectra, quality, slot_order, owners):
    npanel, _, bins = source_spectra.shape
    kept = quality.astype(jnp.float32)[:, None, None]
    receivers = whiten(receiver_spectra) * kept
    receivers = jnp.take(receivers, slot_order[0], axis=0).reshape(-1, 2 * bins)
    sources = whiten(source_spectra).reshape(-1, 2 * bins)
    block_index = lax.axis_index("blk")
    my_owners = lax.dynamic_index_in_dim(owners, block_index, 1, keepdims=False)
    every_panel = lax.all_gather(sources, "cross", axis=0)
    panels = jnp.take(every_panel, my_owners, axis=0)
    slabs = jnp.stack([receivers, passed_along(receivers, "blk", 1)])
    return correlate(panels, slabs)[:, None, None]


def solution(mesh):
    placed = (
        P(("blk", "cross"), None, None),
        P(("blk", "cross"), None, None),
        P(("blk", "cross")),
        P(("blk", "cross"), None),
        P(),
    )
    return jax.shard_map(
        local,
        mesh=mesh,
        in_specs=placed,
        out_specs=P(None, "blk", "cross", None, None, None),
        check_vma=False,
    )
```

time: 306 us -> 155 us (0.51)
  matrix products: 90.8 us -> 0 us
  other arithmetic: 85.6 us -> 10.5 us
  Pallas kernels: 0 us -> 46.9 us
  local copies, waits for them, and re-layouts: 39.7 us -> 7.68 us
    dot_general x32 -> x0, matrix products: 90.8 us -> none  [the longest x16 45.8 us: one_block(): odd = jnp.dot(quadrature, sin_table, preferred_element_type=jnp.float32)]
    pallas_call x0 -> x1, Pallas kernels: none -> 46.9 us  [correlate(): pl.pallas_call(functools.partial(kernel, coarse), grid=(steps, npanel //...]
    convert_element_type x16 -> x0, other arithmetic: 42.7 us -> none  [one_block(): quadrature = quadrature.astype(jnp.bfloat16).reshape(width * nslab, -1)]
    dynamic_update_slice x16 -> x0, other arithmetic: 18.4 us -> none  [correlate(): lagged = lax.map(one_block, blocks)]
    slice x33 -> x0, local copies, waits for them, and re-layouts: 15.2 us -> none  [the longest x16 13 us: one_block(): slab_spec[None, :, 0, :]]
    ppermute x1, waiting for transfers between devices: 0.01 us -> 14 us  [passed_along(): return lax.ppermute(value, axis, pairs)]
    broadcast_in_dim x1 -> x0, other arithmetic: 13.8 us -> none  [local(): return jnp.stack(results)[:, None, None]]
    all_gather x1, waiting for transfers between devices: 73.5 us -> 61.1 us  [local(): every_panel = lax.all_gather(sources, 'cross', axis=0)]
  transfers between devices with their start and end apart: 2 -> 2, of which waited for: 1 -> 2; matrix products, arithmetic and copies ran while one was open for 4% -> 5% of each run, Pallas kernels for 0% -> 0%
where the time goes in v1:
time: 155 us; the launch traced here: 154 us
  waiting for transfers between devices  75.1 us (48%)
  Pallas kernels  46.9 us (30%)
  between operations  13.5 us (9%)
  other arithmetic  10.5 us (7%)
  local copies, waits for them, and re-layouts  7.68 us (5%)
    all_gather x1, waiting for transfers between devices, local(): every_panel = lax.all_gather(sources, 'cross', axis=0)  61.1 us
    pallas_call x1, Pallas kernels, correlate(): pl.pallas_call(functools.partial(kernel, coarse), grid=(steps, npanel //...  46.9 us
    ppermute x1, waiting for transfers between devices, passed_along(): return lax.ppermute(value, axis, pairs)  14 us
    reduce_sum x2, other arithmetic, whiten(): mean_power = jnp.mean(spectra * spectra, axis=(1, 2), keepdims=True)  3.3 us
  transfers between devices with their start and end apart: 2, of which 2 were waited for; matrix products, arithmetic and copies ran while one was open for 5% of the time, Pallas kernels for 0%

profile of v1, /device:TPU:0, one launch (start us, length us, event | category | flops | bytes accessed | tf_op | source)
XLA Modules:
  0.0 154.3 jit_solution(4908205803337610493)
XLA Ops:
  6.5 0.0 all-gather.2.cloned.1.call-start
  6.5 2.3 %multiply_reduce_fusion.1 = f32[128]{0:T(128)S(1)} fusion(f32[128,2,1024]{2,1,0:T(2,128)} %param.8), kind=kLoop, calls=%fused_computation.6 | loop fusion | flops 524160 | bytes 1049088 | tf_op jit(solution)/shard_map/reduce_sum | solution.py:27
  8.8 1.7 %broadcast_multiply_fusion = f32[128,2,1024]{2,1,0:T(2,128)S(1)} fusion(f32[128,2,1024]{2,1,0:T(2,128)} %param.8, f32[128]{0:T(128)S(1)} %add_rsqrt_fusion.1), kind=kLoop, calls=%fused_computation.7 | loop fusion | flops 262144 | bytes 2097664 | tf_op jit(solution)/shard_map/mul | solution.py:28
  10.5 0.0 copy-start.2
  10.5 0.0 copy-start.3
  10.5 0.0 copy-start
  10.5 1.9 %all_gather_reshape.3 = f32[1,128,2048]{2,1,0:T(8,128)} reshape(f32[128,2,1024]{2,1,0:T(2,128)S(1)} %broadcast_multiply_fusion) | data formatting | bytes 2097152 | tf_op jit(solution)/shard_map/all_gather;reshape | solution.py:120
  12.4 0.0 all-gather.2.cloned.1.call-update
  12.4 0.0 copy-done.2
  12.4 0.0 copy-done.3
  12.5 0.0 copy-done
  12.5 1.0 multiply_reduce_fusion
  13.5 0.5 multiply_multiply_fusion
  14.0 1.7 %gather_fusion.1 = f32[128,2,1024]{2,1,0:T(2,128)S(1)} fusion(f32[128,2,1024]{2,1,0:T(2,128)S(1)} %multiply_multiply_fusion, s32[1024]{0:T(1024)S(1)} %pad_clamp_fusion), kind=kCustom, calls=%fused_computation.1 | custom fusion | bytes 2097664 | tf_op jit(solution)/shard_map/jit(_take)/gather | solution.py:116
  15.7 0.3 copy.10
  16.0 0.0 copy-start.1
  16.0 0.1 broadcast_select_fusion.1
  16.2 0.5 collective-permute-start
  16.7 0.9 gather.14
  17.6 0.0 copy-done.1
  17.7 0.2 fusion.1
  17.8 0.2 and_reduce_fusion
  18.0 0.1 broadcast_select_fusion.2
  18.2 14.0 %collective-permute-done = f32[128,2048]{1,0:T(8,128)} collective-permute-done((f32[128,2048]{1,0:T(8,128)S(1)}, f32[128,2048]{1,0:T(8,128)}, u32[]{:S(2)}, u32[]{:S(2)}) %collective-permute-start) | collective-permute-done | bytes 1048608 | tf_op jit(solution)/shard_map/ppermute | solution.py:109
  32.2 2.8 %pad_maximum_fusion.q_ref = f32[2,128,2048]{2,1,0:T(8,128)} fusion(f32[1,128,2048]{2,1,0:T(8,128)} %bitcast.3, f32[1,128,2048]{2,1,0:T(8,128)S(1)} %broadcast_select_fusion.2), kind=kLoop, calls=%fused_computation.2 | loop fusion | flops 524288 | bytes 4194304 | tf_op jit(solution)/shard_map/stack | solution.py:122
  34.9 61.1 %all-gather.2.cloned.1.call-done = f32[4,128,2048]{2,1,0:T(8,128)} async-done(((f32[1,128,2048]{2,1,0:T(8,128)}), f32[4,128,2048]{2,1,0:T(8,128)}) %all-gather.2.cloned.1.call-update) | async-done | bytes 4194320 | tf_op jit(solution)/shard_map/all_gather | solution.py:120
  96.0 2.9 %gather_fusion = f32[2,128,2048]{2,1,0:T(8,128)S(1)} fusion(f32[4,128,2048]{2,1,0:T(8,128)} %all-gather.2.cloned.1.call-done, s32[1024]{0:T(1024)S(1)} %pad_clamp_fusion.1), kind=kCustom, calls=%fused_computation | custom fusion | bytes 4194312 | tf_op jit(solution)/shard_map/jit(_take)/gather | solution.py:121
  98.9 1.6 %broadcast_select_fusion.s_ref = f32[2,128,2048]{2,1,0:T(8,128)} fusion(f32[2,128,2048]{2,1,0:T(8,128)S(1)} %gather_fusion, pred[2]{0:T(512)(128)(4,1)S(1)} %and_reduce_fusion), kind=kLoop, calls=%fused_computation.5 | loop fusion | flops 524288 | bytes 4194306 | tf_op jit(solution)/shard_map/jit(_take)/select_n | solution.py:121
  100.5 46.9 %shard_map.73 = bf16[2,128,128,256]{3,2,1,0:T(8,128)(2,1)} custom-call(f32[2,128,2048]{2,1,0:T(8,128)} %broadcast_select_fusion.s_ref, f32[2,128,2048]{2,1,0:T(8,128)} %pad_maximum_fusion.q_ref, f32[2,16,1024]{2,1,0:T(8,128)} %constant.53.clone.fine_ref, f32[2,8,1024]{2,1,0:T(8,128)} %constant.54.clone.slow_ref), custom_call_target="tpu_custom_call" | custom-call | tf_op jit(solution)/shard_map/pallas_call | solution.py:87
  (7 shorter events, 0.0 us)
Async XLA Ops:
  6.5 89.5 %all-gather.2.cloned.1.call-start = ((), (), s32[]{:S(2)}) async-start(), calls=%async_computation | async-start | bytes 5242880 | tf_op jit(solution)/shard_map/all_gather | solution.py:120
  10.5 1.9 %copy-start.2 = (s32[128]{0:T(128)S(1)}, s32[128]{0:T(128)}, u32[]{:S(2)}) copy-start(s32[128]{0:T(128)} %param.9) | copy-start | bytes 1540
  10.5 1.9 %copy-start.3 = (s32[1,128]{1,0:T(1,128)S(1)}, s32[1,128]{1,0:T(1,128)}, u32[]{:S(2)}) copy-start(s32[1,128]{1,0:T(1,128)} %param.10) | copy-start | bytes 1540
  10.5 2.0 %copy-start = (f32[128,2,1024]{2,1,0:T(2,128)S(1)}, f32[128,2,1024]{2,1,0:T(2,128)}, u32[]{:S(2)}) copy-start(f32[128,2,1024]{2,1,0:T(2,128)} %param.7) | copy-start | bytes 3145732
  16.0 1.6 %copy-start.1 = (s32[2,8]{1,0:T(2,128)S(1)}, s32[2,8]{1,0:T(2,128)}, u32[]{:S(2)}) copy-start(s32[2,8]{1,0:T(2,128)} %param.11) | copy-start | bytes 196
  16.2 16.0 %collective-permute-start = (f32[128,2048]{1,0:T(8,128)S(1)}, f32[128,2048]{1,0:T(8,128)}, u32[]{:S(2)}, u32[]{:S(2)}) collective-permute-start(f32[128,2048]{1,0:T(8,128)S(1)} %broadcast_select_fusion.1), channel_id=1, source_target_pairs={{0,4},{4,8},{8,12},{12,16},{16,20},{20,24},{24,28},{28,0},{1,5},{5... | collective-permute-start | bytes 3145736 | tf_op jit(solution)/shard_map/ppermute | solution.py:109
Sparse Core Ops, SparseCore 0:
  12.5 83.4 all-gather.1

commit v2 on v1

v2 whole, which is shorter than its diff:
```python
import functools
import math

import jax
import jax.numpy as jnp
import numpy as np
from jax import lax
from jax.experimental import pallas as pl
from jax.experimental.pallas import tpu as pltpu
from jax.sharding import PartitionSpec as P

L = 256
STEPS = 2
FINE = 16
PIECE = 8
HOP = 2
MESH = pl.DeviceIdType.MESH


def phase_tables(bins, coarse):
    bin_index = np.arange(bins, dtype=np.float64)[None, :]
    fine_angle = np.pi / bins * (np.arange(FINE)[:, None] + 0.5) * bin_index
    coarse_angle = np.pi / bins * (FINE * np.arange(coarse)[:, None]) * bin_index
    fine = np.stack([np.cos(fine_angle), np.sin(fine_angle)])
    slow = np.stack([np.cos(coarse_angle), np.sin(coarse_angle)]) / bins
    return jnp.asarray(fine, jnp.float32), jnp.asarray(slow, jnp.float32)


def whiten(spectra):
    mean_power = jnp.mean(spectra * spectra, axis=(1, 2), keepdims=True)
    return spectra * lax.rsqrt(mean_power + 1e-06)


def build_columns(slab, slow_ref, w_ref):
    bins = slow_ref.shape[2]
    slots = slab.shape[0]
    real, imag = slab[:, :bins], slab[:, bins:]
    for a in range(slow_ref.shape[1]):
        c, s = slow_ref[0, a : a + 1, :], slow_ref[1, a : a + 1, :]
        rc, rs, ic, is_ = real * c, real * s, imag * c, imag * s
        rows = slice(a * slots, (a + 1) * slots)
        w_ref[0, rows, :bins] = (rc + is_).astype(jnp.bfloat16)
        w_ref[0, rows, bins:] = (ic - rs).astype(jnp.bfloat16)
        w_ref[1, rows, :bins] = (rc - is_).astype(jnp.bfloat16)
        w_ref[1, rows, bins:] = (ic + rs).astype(jnp.bfloat16)


def build_rows(panel, fine_ref, x_ref):
    bins = fine_ref.shape[2]
    c, s = fine_ref[0], fine_ref[1]
    for p in range(panel.shape[0]):
        real, imag = panel[p : p + 1, :bins], panel[p : p + 1, bins:]
        rc, rs, ic, is_ = real * c, real * s, imag * c, imag * s
        rows = slice(p * FINE, (p + 1) * FINE)
        x_ref[0, rows, :bins] = (rc - is_).astype(jnp.bfloat16)
        x_ref[0, rows, bins:] = (rs + ic).astype(jnp.bfloat16)
        x_ref[1, rows, :bins] = (rc + is_).astype(jnp.bfloat16)
        x_ref[1, rows, bins:] = (ic - rs).astype(jnp.bfloat16)


def product(x_ref, w_ref, out_ref, sign, channels, slots, coarse):
    half = coarse * FINE
    found = lax.dot_general(
        x_ref[sign], w_ref[sign], (((1,), (1,)), ((), ())), preferred_element_type=jnp.float32
    )
    for p in range(channels):
        part = found[p * FINE : (p + 1) * FINE]
        lags = jnp.concatenate([part[:, a * slots : (a + 1) * slots] for a in range(coarse)], axis=0)
        out_ref[p, :, sign * half : (sign + 1) * half] = lags.T.astype(jnp.bfloat16)


def kernel(
    coarse, channels, count, ring, owner_ref, own_ref, q_ref, fine_ref, slow_ref, out_ref,
    w_ref, x_ref, low, high, near, low_send, low_recv, high_send, high_recv, q_send, q_recv,
):
    step, block = pl.program_id(0), pl.program_id(1)
    npanel, slots = own_ref.shape[0], q_ref.shape[0]
    per_step = npanel // PIECE
    total = STEPS * per_step
    per_block = channels // PIECE
    blocks = npanel // channels
    me, spot = lax.axis_index("cross"), lax.axis_index("blk")
    has_low, has_high = me > 0, me < count - 1
    following, previous = lax.rem(spot + 1, ring), lax.rem(spot + ring - 1, ring)

    def own_rows(j):
        return pl.ds(pl.multiple_of(lax.rem(j, per_step) * PIECE, PIECE), PIECE)

    def upward(j, source):
        return pltpu.make_async_remote_copy(
            src_ref=source, dst_ref=low.at[j], send_sem=low_send.at[j], recv_sem=low_recv.at[j],
            device_id={"blk": spot, "cross": me + 1}, device_id_type=MESH,
        )

    def downward(j, source):
        return pltpu.make_async_remote_copy(
            src_ref=source, dst_ref=high.at[j], send_sem=high_send.at[j], recv_sem=high_recv.at[j],
            device_id={"blk": spot, "cross": me - 1}, device_id_type=MESH,
        )

    def slab_copy():
        return pltpu.make_async_remote_copy(
            src_ref=q_ref, dst_ref=near, send_sem=q_send.at[0], recv_sem=q_recv.at[0],
            device_id={"blk": following, "cross": me}, device_id_type=MESH,
        )

    def relay(t):
        up, down = t - HOP * (me - 1), t - HOP * (count - 2 - me)
        up_on = has_low & (up >= 0) & (up < total)
        down_on = has_high & (down >= 0) & (down < total)

        @pl.when(up_on)
        def _():
            upward(up, low.at[up]).wait_recv()
            mine = owner_ref[up // per_step] == me
            low[up] = jnp.where(mine, own_ref[own_rows(up), :], low[up])

        @pl.when(down_on)
        def _():
            downward(down, high.at[down]).wait_recv()
            mine = owner_ref[down // per_step] == me
            high[down] = jnp.where(mine, own_ref[own_rows(down), :], high[down])

        @pl.when(up_on & has_high)
        def _():
            upward(up, low.at[up]).start()

        @pl.when(down_on & has_low)
        def _():
            downward(down, high.at[down]).start()

    lead = HOP * (count - 2) + per_block

    @pl.when((step == 0) & (block == 0))
    def _():
        barrier = pltpu.get_barrier_semaphore()
        pl.semaphore_signal(barrier, inc=1, device_id={"blk": following, "cross": me}, device_id_type=MESH)
        pl.semaphore_signal(barrier, inc=1, device_id={"blk": previous, "cross": me}, device_id_type=MESH)

        @pl.when(has_low)
        def _():
            pl.semaphore_signal(barrier, inc=1, device_id={"blk": spot, "cross": me - 1}, device_id_type=MESH)

        @pl.when(has_high)
        def _():
            pl.semaphore_signal(barrier, inc=1, device_id={"blk": spot, "cross": me + 1}, device_id_type=MESH)

        pl.semaphore_wait(barrier, 2 + has_low.astype(jnp.int32) + has_high.astype(jnp.int32))

        @pl.when(me == 0)
        def _():
            @pl.loop(0, total)
            def _(j):
                upward(j, own_ref.at[own_rows(j), :]).start()

        @pl.when(me == count - 1)
        def _():
            @pl.loop(0, total)
            def _(j):
                downward(j, own_ref.at[own_rows(j), :]).start()

        slab_copy().start()

        @pl.when(me == 0)
        def _():
            @pl.loop(0, total)
            def _(j):
                low[j] = own_ref[own_rows(j), :]

        @pl.when(me == count - 1)
        def _():
            @pl.loop(0, total)
            def _(j):
                high[j] = own_ref[own_rows(j), :]

        build_columns(q_ref[...], slow_ref, w_ref)

        @pl.loop(0, lead)
        def _(t):
            relay(t)

    @pl.when((step == 1) & (block == 0))
    def _():
        slab_copy().wait()
        build_columns(near[...], slow_ref, w_ref)

    now = (step * blocks + block) * per_block
    above = owner_ref[step] > me
    panel = jnp.concatenate([jnp.where(above, high[now + j], low[now + j]) for j in range(per_block)], axis=0)
    mean_power = jnp.mean(panel * panel, axis=1, keepdims=True)
    build_rows(panel * lax.rsqrt(mean_power + 1e-06), fine_ref, x_ref)
    for sign in range(2):
        product(x_ref, w_ref, out_ref.at[0], sign, channels, slots, coarse)
        for extra in range(per_block // 2):
            relay(now + lead + sign * (per_block // 2) + extra)

    @pl.when((step == STEPS - 1) & (block == blocks - 1))
    def _():
        @pl.when(has_high)
        def _():
            @pl.loop(0, total)
            def _(j):
                upward(j, low.at[j]).wait_send()

        @pl.when(has_low)
        def _():
            @pl.loop(0, total)
            def _(j):
                downward(j, high.at[j]).wait_send()


def correlate(owners, sources, slab, count, ring, channels=16):
    npanel, width = sources.shape
    nslab = slab.shape[0]
    coarse = L // 2 // FINE
    fine, slow = phase_tables(width // 2, coarse)
    total = STEPS * npanel // PIECE
    whole = pl.BlockSpec(memory_space=pltpu.VMEM)
    pieces = pltpu.VMEM((total, PIECE, width), jnp.float32)
    many = pltpu.SemaphoreType.DMA((total,))
    one = pltpu.SemaphoreType.DMA((1,))
    return pl.pallas_call(
        functools.partial(kernel, coarse, channels, count, ring),
        grid=(STEPS, npanel // channels),
        in_specs=[pl.BlockSpec(memory_space=pltpu.SMEM), whole, whole, whole, whole],
        out_specs=pl.BlockSpec((1, channels, nslab, L), lambda s, i: (s, i, 0, 0)),
        out_shape=jax.ShapeDtypeStruct((STEPS, npanel, nslab, L), jnp.bfloat16),
        scratch_shapes=[
            pltpu.VMEM((2, coarse * nslab, width), jnp.bfloat16),
            pltpu.VMEM((2, channels * FINE, width), jnp.bfloat16),
            pieces, pieces, pltpu.VMEM((nslab, width), jnp.float32),
            many, many, many, many, one, one,
        ],
        compiler_params=pltpu.CompilerParams(
            vmem_limit_bytes=56 << 20, collective_id=0, has_side_effects=True
        ),
    )(owners, sources, slab, fine, slow)


def local(receiver_spectra, source_spectra, quality, slot_order, owners):
    bins = source_spectra.shape[2]
    kept = quality.astype(jnp.float32)[:, None, None]
    receivers = whiten(receiver_spectra) * kept
    receivers = jnp.take(receivers, slot_order[0], axis=0).reshape(-1, 2 * bins)
    sources = source_spectra.reshape(-1, 2 * bins)
    my_owners = lax.dynamic_index_in_dim(owners, lax.axis_index("blk"), 1, keepdims=False)
    count, ring = lax.axis_size("cross"), lax.axis_size("blk")
    return correlate(my_owners, sources, receivers, count, ring)[:, None, None]


def solution(mesh):
    placed = (
        P(("blk", "cross"), None, None),
        P(("blk", "cross"), None, None),
        P(("blk", "cross")),
        P(("blk", "cross"), None),
        P(),
    )
    return jax.shard_map(
        local,
        mesh=mesh,
        in_specs=placed,
        out_specs=P(None, "blk", "cross", None, None, None),
        check_vma=False,
    )
```

time: 155 us -> 106 us (0.68)
  waiting for transfers between devices: 75.1 us -> 0 us
  Pallas kernels: 46.9 us -> 79 us
  between operations: 13.5 us -> 0.03 us
  local copies, waits for them, and re-layouts: 7.68 us -> 20 us
  other arithmetic: 10.5 us -> 7.07 us
    all_gather x1 -> x0, waiting for transfers between devices: 61.1 us -> none  [local(): every_panel = lax.all_gather(sources, 'cross', axis=0)]
    pallas_call x1, Pallas kernels: 46.9 us -> 79 us  [correlate(): pl.pallas_call(functools.partial(kernel, coarse, channels, count, ring),...]
    unnamed x9 -> x5, local copies, waits for them, and re-layouts: 0.37 us -> 17.6 us
    ppermute x1 -> x0, waiting for transfers between devices: 14 us -> none  [passed_along(): return lax.ppermute(value, axis, pairs)]
    gather x1 -> x0, local copies, waits for them, and re-layouts: 2.87 us -> none  [local(): panels = jnp.take(every_panel, my_owners, axis=0)]
    another operation x1 -> x0, other arithmetic: 2.75 us -> none  [local(): slabs = jnp.stack([receivers, passed_along(receivers, 'blk', 1)])]
    another operation x1 -> x0, local copies, waits for them, and re-layouts: 1.87 us -> none  [local(): every_panel = lax.all_gather(sources, 'cross', axis=0)]
    select_n x2 -> x0, other arithmetic: 1.83 us -> none  [local(): panels = jnp.take(every_panel, my_owners, axis=0)]
  transfers between devices with their start and end apart: 2 -> 0, of which waited for: 2 -> 0; matrix products, arithmetic and copies ran while one was open for 5% -> 0% of each run, Pallas kernels for 0% -> 0%
where the time goes in v2:
time: 106 us
  Pallas kernels  79 us (75%)
  local copies, waits for them, and re-layouts  20 us (19%)
  other arithmetic  7.07 us (7%)
    pallas_call x1, Pallas kernels, correlate(): pl.pallas_call(functools.partial(kernel, coarse, channels, count, ring),...  79 us
    unnamed x5, local copies, waits for them, and re-layouts  17.6 us
    reduce_sum x1, other arithmetic, whiten(): mean_power = jnp.mean(spectra * spectra, axis=(1, 2), keepdims=True)  2.26 us

profile of v2, /device:TPU:0, one launch (start us, length us, event | category | flops | bytes accessed | tf_op | source)
XLA Modules:
  0.0 106.1 jit_solution(11234033452345699290)
XLA Ops:
  0.0 0.0 copy-start
  0.0 0.7 copy-done
  0.7 0.7 dynamic-slice_reduce_fusion.owner_ref
  1.4 0.7 convert_element_type.3
  2.0 2.3 %multiply_reduce_fusion = f32[128]{0:T(128)S(1)} fusion(f32[128,2,1024]{2,1,0:T(2,128)} %param.7), kind=kLoop, calls=%fused_computation.2 | loop fusion | flops 524160 | bytes 1049088 | tf_op jit(solution)/shard_map/reduce_sum | solution.py:30
  4.3 0.7 fusion
  5.0 0.7 compare_and_fusion
  5.6 1.7 %multiply_multiply_fusion = f32[128,2,1024]{2,1,0:T(2,128)S(1)} fusion(f32[128,2,1024]{2,1,0:T(2,128)} %param.7, f32[128]{0:T(128)S(1)} %convert_element_type.3, f32[128]{0:T(128)S(1)} %add_rsqrt_fusion), kind=kLoop, calls=%fused_computation.1 | loop fusion | flops 524288 | bytes 2098176 | tf_op jit(solution)/shard_map/mul | solution.py:243
  7.3 1.7 %gather_fusion = f32[128,2,1024]{2,1,0:T(2,128)S(1)} fusion(f32[128,2,1024]{2,1,0:T(2,128)S(1)} %multiply_multiply_fusion, s32[1024]{0:T(1024)S(1)} %pad_clamp_fusion), kind=kCustom, calls=%fused_computation | custom fusion | bytes 2097664 | tf_op jit(solution)/shard_map/jit(_take)/gather | solution.py:244
  9.0 0.3 copy.10
  9.4 1.1 %broadcast_select_fusion.q_ref = f32[128,2048]{1,0:T(8,128)} fusion(f32[128,2048]{1,0:T(8,128)S(1)} %bitcast.16, pred[128]{0:T(512)(128)(4,1)S(1)} %compare_and_fusion), kind=kLoop, calls=%fused_computation.3 | loop fusion | flops 262144 | bytes 2097280 | tf_op jit(solution)/shard_map/jit(_take)/select_n | solution.py:244
  10.5 2.5 %copy.9 = f32[16,8,2,1024]{3,1,2,0:T(8,128)} copy(f32[16,8,2,1024]{3,2,1,0:T(2,128)} %bitcast.17) | data formatting | bytes 2097152
  13.0 79.0 %shard_map.73 = bf16[2,128,128,256]{3,2,1,0:T(8,128)(2,1)} custom-call(s32[2]{0:T(128)} %dynamic-slice_reduce_fusion.owner_ref, f32[128,2048]{1,0:T(8,128)} %bitcast.14, f32[128,2048]{1,0:T(8,128)} %broadcast_select_fusion.q_ref, f32[2,16,1024]{2,1,0:T(8,128)} %constant.38.clone.fine_ref, f32[2,8,1024]{2,1,0:T(8,128)} %constant.39.clone.slow_ref), custom_call_target="tpu_custom_call" | custom-call | tf_op jit(solution)/shard_map/pallas_call | solution.py:222
  92.1 14.1 %copy.12 = bf16[2,1,1,128,128,256]{5,4,3,2,1,0:T(8,128)(2,1)} copy(bf16[2,1,1,128,128,256]{5,4,3,2,1,0:T(8,128)(2,1)} %bitcast.13) | data formatting | bytes 33554432
  (2 shorter events, 0.0 us)
Async XLA Ops:
  0.0 0.7 copy-start

commit v3 on v2

--- a/solution.py
+++ b/solution.py
@@ -14,6 +14,7 @@
 FINE = 16
 PIECE = 8
 HOP = 2
+GROUP = 4
 MESH = pl.DeviceIdType.MESH
 
 
@@ -26,9 +27,16 @@
     return jnp.asarray(fine, jnp.float32), jnp.asarray(slow, jnp.float32)
 
 
-def whiten(spectra):
-    mean_power = jnp.mean(spectra * spectra, axis=(1, 2), keepdims=True)
-    return spectra * lax.rsqrt(mean_power + 1e-06)
+def ordered(spectra, kept, slot_order):
+    mean_power = jnp.mean(spectra * spectra, axis=1, keepdims=True)
+    scaled = spectra * lax.rsqrt(mean_power + 1e-06) * kept
+    coarse_part = scaled.astype(jnp.bfloat16)
+    fine_part = (scaled - coarse_part.astype(jnp.float32)).astype(jnp.bfloat16)
+    count = spectra.shape[0]
+    picks = slot_order == lax.broadcasted_iota(jnp.int32, (count, count), 1)
+    picks = jnp.where(picks, 1.0, 0.0).astype(jnp.bfloat16)
+    first = jnp.dot(picks, coarse_part, preferred_element_type=jnp.float32)
+    return first + jnp.dot(picks, fine_part, preferred_element_type=jnp.float32)
 
 
 def build_columns(slab, slow_ref, w_ref):
@@ -70,8 +78,8 @@
 
 
 def kernel(
-    coarse, channels, count, ring, owner_ref, own_ref, q_ref, fine_ref, slow_ref, out_ref,
-    w_ref, x_ref, low, high, near, low_send, low_recv, high_send, high_recv, q_send, q_recv,
+    coarse, channels, count, ring, owner_ref, own_ref, raw_ref, kept_ref, order_ref, fine_ref, slow_ref,
+    out_ref, rows_ref, slabs_ref, w_ref, x_ref, q_ref, low, high, near, low_send, low_recv, high_send, high_recv, q_send, q_recv,
 ):
     step, block = pl.program_id(0), pl.program_id(1)
     npanel, slots = own_ref.shape[0], q_ref.shape[0]
@@ -159,21 +167,22 @@
             def _(j):
                 downward(j, own_ref.at[own_rows(j), :]).start()
 
+        @pl.when(me == 0)
+        def _():
+            @pl.loop(0, total)
+            def _(j):
+                low[j] = own_ref[own_rows(j), :]
+
+        @pl.when(me == count - 1)
+        def _():
+            @pl.loop(0, total)
+            def _(j):
+                high[j] = own_ref[own_rows(j), :]
+
+        q_ref[...] = ordered(raw_ref[...], kept_ref[...], order_ref[...])
+        slabs_ref[0] = q_ref[...]
+        build_columns(q_ref[...], slow_ref, w_ref)
         slab_copy().start()
-
-        @pl.when(me == 0)
-        def _():
-            @pl.loop(0, total)
-            def _(j):
-                low[j] = own_ref[own_rows(j), :]
-
-        @pl.when(me == count - 1)
-        def _():
-            @pl.loop(0, total)
-            def _(j):
-                high[j] = own_ref[own_rows(j), :]
-
-        build_columns(q_ref[...], slow_ref, w_ref)
 
         @pl.loop(0, lead)
         def _(t):
@@ -182,15 +191,29 @@
     @pl.when((step == 1) & (block == 0))
     def _():
         slab_copy().wait()
+        slabs_ref[1] = near[...]
         build_columns(near[...], slow_ref, w_ref)
 
     now = (step * blocks + block) * per_block
     above = owner_ref[step] > me
     panel = jnp.concatenate([jnp.where(above, high[now + j], low[now + j]) for j in range(per_block)], axis=0)
     mean_power = jnp.mean(panel * panel, axis=1, keepdims=True)
-    build_rows(panel * lax.rsqrt(mean_power + 1e-06), fine_ref, x_ref)
+    panel = panel * lax.rsqrt(mean_power + 1e-06)
+    later = lax.rem(block, GROUP) == GROUP - 1
+
+    @pl.when(later)
+    def _():
+        rows_ref[0] = panel
+
+    @pl.when(jnp.logical_not(later))
+    def _():
+        build_rows(panel, fine_ref, x_ref)
+
     for sign in range(2):
-        product(x_ref, w_ref, out_ref.at[0], sign, channels, slots, coarse)
+        @pl.when(jnp.logical_not(later))
+        def _():
+            product(x_ref, w_ref, out_ref.at[0], sign, channels, slots, coarse)
+
         for extra in range(per_block // 2):
             relay(now + lead + sign * (per_block // 2) + extra)
 
@@ -209,43 +232,84 @@
                 downward(j, high.at[j]).wait_send()
 
 
-def correlate(owners, sources, slab, count, ring, channels=16):
+def finish(coarse, done_ref, rows_ref, slab_ref, fine_ref, slow_ref, out_ref, w_ref, x_ref):
+    channels, slots = rows_ref.shape[1], slab_ref.shape[1]
+
+    @pl.when(pl.program_id(1) == 0)
+    def _():
+        build_columns(slab_ref[0], slow_ref, w_ref)
+
+    build_rows(rows_ref[0], fine_ref, x_ref)
+    out_ref[: GROUP - 1] = done_ref[...]
+    for sign in range(2):
+        product(x_ref, w_ref, out_ref.at[GROUP - 1], sign, channels, slots, coarse)
+
+
+def correlate(owners, sources, raw, kept, order, count, ring, channels=16):
     npanel, width = sources.shape
-    nslab = slab.shape[0]
+    nslab = raw.shape[0]
     coarse = L // 2 // FINE
     fine, slow = phase_tables(width // 2, coarse)
     total = STEPS * npanel // PIECE
+    blocks = npanel // channels
+    groups = blocks // GROUP
     whole = pl.BlockSpec(memory_space=pltpu.VMEM)
     pieces = pltpu.VMEM((total, PIECE, width), jnp.float32)
+    slab = pltpu.VMEM((nslab, width), jnp.float32)
     many = pltpu.SemaphoreType.DMA((total,))
     one = pltpu.SemaphoreType.DMA((1,))
-    return pl.pallas_call(
+    columns = pltpu.VMEM((2, coarse * nslab, width), jnp.bfloat16)
+    rotated = pltpu.VMEM((2, channels * FINE, width), jnp.bfloat16)
+    kept_blocks = groups * (GROUP - 1)
+
+    def kept_index(s, i):
+        return (s * kept_blocks + i // GROUP * (GROUP - 1) + jnp.minimum(i % GROUP, GROUP - 2), 0, 0, 0)
+
+    done, rows, slabs = pl.pallas_call(
         functools.partial(kernel, coarse, channels, count, ring),
-        grid=(STEPS, npanel // channels),
-        in_specs=[pl.BlockSpec(memory_space=pltpu.SMEM), whole, whole, whole, whole],
-        out_specs=pl.BlockSpec((1, channels, nslab, L), lambda s, i: (s, i, 0, 0)),
-        out_shape=jax.ShapeDtypeStruct((STEPS, npanel, nslab, L), jnp.bfloat16),
-        scratch_shapes=[
-            pltpu.VMEM((2, coarse * nslab, width), jnp.bfloat16),
-            pltpu.VMEM((2, channels * FINE, width), jnp.bfloat16),
-            pieces, pieces, pltpu.VMEM((nslab, width), jnp.float32),
-            many, many, many, many, one, one,
+        grid=(STEPS, blocks),
+        in_specs=[pl.BlockSpec(memory_space=pltpu.SMEM)] + [whole] * 6,
+        out_specs=[
+            pl.BlockSpec((1, channels, nslab, L), kept_index),
+            pl.BlockSpec((1, channels, width), lambda s, i: (s * groups + i // GROUP, 0, 0)),
+            whole,
         ],
+        out_shape=[
+            jax.ShapeDtypeStruct((STEPS * kept_blocks, channels, nslab, L), jnp.bfloat16),
+            jax.ShapeDtypeStruct((STEPS * groups, channels, width), jnp.float32),
+            jax.ShapeDtypeStruct((STEPS, nslab, width), jnp.float32),
+        ],
+        scratch_shapes=[columns, rotated, slab, pieces, pieces, slab, many, many, many, many, one, one],
         compiler_params=pltpu.CompilerParams(
             vmem_limit_bytes=56 << 20, collective_id=0, has_side_effects=True
         ),
-    )(owners, sources, slab, fine, slow)
+    )(owners, sources, raw, kept, order, fine, slow)
+    return pl.pallas_call(
+        functools.partial(finish, coarse),
+        grid=(STEPS, groups),
+        in_specs=[
+            pl.BlockSpec((GROUP - 1, channels, nslab, L), lambda s, g: (s * groups + g, 0, 0, 0)),
+            pl.BlockSpec((1, channels, width), lambda s, g: (s * groups + g, 0, 0)),
+            pl.BlockSpec((1, nslab, width), lambda s, g: (s, 0, 0)),
+            pl.BlockSpec(fine.shape, lambda s, g: (0, 0, 0)),
+            pl.BlockSpec(slow.shape, lambda s, g: (0, 0, 0)),
+        ],
+        out_specs=pl.BlockSpec((GROUP, channels, nslab, L), lambda s, g: (s * groups + g, 0, 0, 0)),
+        out_shape=jax.ShapeDtypeStruct((STEPS * blocks, channels, nslab, L), jnp.bfloat16),
+        scratch_shapes=[columns, rotated],
+        compiler_params=pltpu.CompilerParams(vmem_limit_bytes=56 << 20),
+    )(done, rows, slabs, fine, slow).reshape(STEPS, npanel, nslab, L)
 
 
 def local(receiver_spectra, source_spectra, quality, slot_order, owners):
     bins = source_spectra.shape[2]
-    kept = quality.astype(jnp.float32)[:, None, None]
-    receivers = whiten(receiver_spectra) * kept
-    receivers = jnp.take(receivers, slot_order[0], axis=0).reshape(-1, 2 * bins)
+    raw = receiver_spectra.reshape(-1, 2 * bins)
     sources = source_spectra.reshape(-1, 2 * bins)
+    kept = quality.astype(jnp.float32)[:, None]
+    order = slot_order[0][:, None]
     my_owners = lax.dynamic_index_in_dim(owners, lax.axis_index("blk"), 1, keepdims=False)
     count, ring = lax.axis_size("cross"), lax.axis_size("blk")
-    return correlate(my_owners, sources, receivers, count, ring)[:, None, None]
+    return correlate(my_owners, sources, raw, kept, order, count, ring)[:, None, None]
 
 
 def solution(mesh):

time: 106 us -> 108 us (1.019)
  Pallas kernels: 79 us -> 98.3 us
  local copies, waits for them, and re-layouts: 20 us -> 8.61 us
  other arithmetic: 7.07 us -> 0.66 us
    pallas_call x0 -> x1, Pallas kernels: none -> 20.6 us  [correlate(): pl.pallas_call(functools.partial(finish, coarse), grid=(STEPS, groups), i...]
    unnamed x5 -> x4, local copies, waits for them, and re-layouts: 17.6 us -> 5.75 us
    reduce_sum x1 -> x0, other arithmetic: 2.26 us -> none  [whiten(): mean_power = jnp.mean(spectra * spectra, axis=(1, 2), keepdims=True)]
    select_n x2 -> x0, other arithmetic: 1.79 us -> none  [local(): receivers = jnp.take(receivers, slot_order[0], axis=0).reshape(-1, 2 * bins)]
    mul x1 -> x0, other arithmetic: 1.69 us -> none  [local(): receivers = whiten(receiver_spectra) * kept]
    gather x1 -> x0, local copies, waits for them, and re-layouts: 1.68 us -> none  [local(): receivers = jnp.take(receivers, slot_order[0], axis=0).reshape(-1, 2 * bins)]
    another operation x0 -> x1, local copies, waits for them, and re-layouts: none -> 1.37 us  [local(): order = slot_order[0][:, None]]
    pallas_call x1, Pallas kernels: 79 us -> 77.7 us  [correlate(): pl.pallas_call(functools.partial(kernel, coarse, channels, count, ring),...]
where the time goes in v3:
time: 108 us
  Pallas kernels  98.3 us (91%)
  local copies, waits for them, and re-layouts  8.61 us (8%)
    pallas_call x1, Pallas kernels, correlate(): pl.pallas_call(functools.partial(kernel, coarse, channels, count, ring),...  77.7 us
    pallas_call x1, Pallas kernels, correlate(): pl.pallas_call(functools.partial(finish, coarse), grid=(STEPS, groups), i...  20.6 us
    unnamed x4, local copies, waits for them, and re-layouts  5.75 us

profile of v3, /device:TPU:0, one launch (start us, length us, event | category | flops | bytes accessed | tf_op | source)
XLA Modules:
  0.0 107.6 jit_solution(9530375852160085522)
XLA Ops:
  0.0 0.0 copy-start
  0.0 0.7 copy-done
  0.7 0.8 dynamic-slice_reduce_fusion.owner_ref
  1.4 0.7 convert_bitcast_fusion
  2.1 0.7 copy.8.kept_ref
  2.8 1.4 %copy.9.order_ref = s32[128,1]{1,0:T(8,128)} copy(s32[128,1]{0,1:T(1,128)} %bitcast.14) | data formatting | bytes 1024 | tf_op jit(solution)/shard_map/broadcast_in_dim;squeeze | solution.py:309
  4.2 2.5 %copy.12 = f32[16,8,2,1024]{3,1,2,0:T(8,128)} copy(f32[16,8,2,1024]{3,2,1,0:T(2,128)} %bitcast.12) | data formatting | bytes 2097152
  6.7 2.5 %copy.11 = f32[16,8,2,1024]{3,1,2,0:T(8,128)} copy(f32[16,8,2,1024]{3,2,1,0:T(2,128)} %bitcast.13) | data formatting | bytes 2097152
  9.3 77.7 %shard_map.73 = (bf16[12,16,128,256]{3,2,1,0:T(8,128)(2,1)}, f32[4,16,2048]{2,1,0:T(8,128)}, f32[2,128,2048]{2,1,0:T(8,128)}) custom-call(s32[2]{0:T(128)} %dynamic-slice_reduce_fusion.owner_ref, f32[128,2048]{1,0:T(8,128)} %bitcast.11, f32[128,2048]{1,0:T(8,128)} %bitcast.10, f32[128,1]{1,0:T(8,128)} %copy.8.kept_ref, s32[128,1]{1,0:T(8,128)} %copy.9.order_ref, ...), custom_call_target="tpu_custom_call" | custom-call | tf_op jit(solution)/shard_map/pallas_call | solution.py:268
  87.0 20.6 %shard_map.74 = bf16[16,16,128,256]{3,2,1,0:T(8,128)(2,1)} custom-call(bf16[12,16,128,256]{3,2,1,0:T(8,128)(2,1)} %get-tuple-element.8.done_ref, f32[4,16,2048]{2,1,0:T(8,128)} %get-tuple-element.9.rows_ref, f32[2,128,2048]{2,1,0:T(8,128)} %get-tuple-element.10.slab_ref, f32[2,16,1024]{2,1,0:T(8,128)} %constant.16.clone.fine_ref, ...), custom_call_target="tpu_custom_call" | custom-call | tf_op jit(solution)/shard_map/pallas_call | solution.py:287
Async XLA Ops:
  0.0 0.7 copy-start

commit v4 on v3

--- a/solution.py
+++ b/solution.py
@@ -13,7 +13,7 @@
 STEPS = 2
 FINE = 16
 PIECE = 8
-HOP = 2
+HOP = 3
 GROUP = 4
 MESH = pl.DeviceIdType.MESH
 
@@ -181,10 +181,15 @@
 
         q_ref[...] = ordered(raw_ref[...], kept_ref[...], order_ref[...])
         slabs_ref[0] = q_ref[...]
+
+        @pl.loop(0, per_block)
+        def _(t):
+            relay(t)
+
         build_columns(q_ref[...], slow_ref, w_ref)
         slab_copy().start()
 
-        @pl.loop(0, lead)
+        @pl.loop(per_block, lead)
         def _(t):
             relay(t)
 

time: 108 us -> 102 us (0.944)
  Pallas kernels: 98.3 us -> 92.2 us
    pallas_call x1, Pallas kernels: 77.7 us -> 71.5 us  [correlate(): pl.pallas_call(functools.partial(kernel, coarse, channels, count, ring),...]
where the time goes in v4:
time: 102 us; the launch traced here: 101 us
  Pallas kernels  92.2 us (90%)
  local copies, waits for them, and re-layouts  8.61 us (8%)
    pallas_call x1, Pallas kernels, correlate(): pl.pallas_call(functools.partial(kernel, coarse, channels, count, ring),...  71.5 us
    pallas_call x1, Pallas kernels, correlate(): pl.pallas_call(functools.partial(finish, coarse), grid=(STEPS, groups), i...  20.6 us
    unnamed x4, local copies, waits for them, and re-layouts  5.75 us

profile of v4, /device:TPU:0, one launch (start us, length us, event | category | flops | bytes accessed | tf_op | source)
XLA Modules:
  0.0 101.4 jit_solution(12419997368429952538)
XLA Ops:
  0.0 0.0 copy-start
  0.0 0.7 copy-done
  0.7 0.8 dynamic-slice_reduce_fusion.owner_ref
  1.4 0.7 convert_bitcast_fusion
  2.1 0.7 copy.8.kept_ref
  2.8 1.4 %copy.9.order_ref = s32[128,1]{1,0:T(8,128)} copy(s32[128,1]{0,1:T(1,128)} %bitcast.14) | data formatting | bytes 1024 | tf_op jit(solution)/shard_map/broadcast_in_dim;squeeze | solution.py:314
  4.2 2.5 %copy.12 = f32[16,8,2,1024]{3,1,2,0:T(8,128)} copy(f32[16,8,2,1024]{3,2,1,0:T(2,128)} %bitcast.12) | data formatting | bytes 2097152
  6.7 2.5 %copy.11 = f32[16,8,2,1024]{3,1,2,0:T(8,128)} copy(f32[16,8,2,1024]{3,2,1,0:T(2,128)} %bitcast.13) | data formatting | bytes 2097152
  9.3 71.5 %shard_map.73 = (bf16[12,16,128,256]{3,2,1,0:T(8,128)(2,1)}, f32[4,16,2048]{2,1,0:T(8,128)}, f32[2,128,2048]{2,1,0:T(8,128)}) custom-call(s32[2]{0:T(128)} %dynamic-slice_reduce_fusion.owner_ref, f32[128,2048]{1,0:T(8,128)} %bitcast.11, f32[128,2048]{1,0:T(8,128)} %bitcast.10, f32[128,1]{1,0:T(8,128)} %copy.8.kept_ref, s32[128,1]{1,0:T(8,128)} %copy.9.order_ref, ...), custom_call_target="tpu_custom_call" | custom-call | tf_op jit(solution)/shard_map/pallas_call | solution.py:273
  80.8 20.6 %shard_map.74 = bf16[16,16,128,256]{3,2,1,0:T(8,128)(2,1)} custom-call(bf16[12,16,128,256]{3,2,1,0:T(8,128)(2,1)} %get-tuple-element.8.done_ref, f32[4,16,2048]{2,1,0:T(8,128)} %get-tuple-element.9.rows_ref, f32[2,128,2048]{2,1,0:T(8,128)} %get-tuple-element.10.slab_ref, f32[2,16,1024]{2,1,0:T(8,128)} %constant.16.clone.fine_ref, ...), custom_call_target="tpu_custom_call" | custom-call | tf_op jit(solution)/shard_map/pallas_call | solution.py:292
Async XLA Ops:
  0.0 0.7 copy-start
